TPU v7x, 256 devices: a whole 4x4x8 slice. The times are simulated.
256 devices in a mesh: stream: 4 (over x), seq: 64 (over z, y, core).
Axes of the slice: x: 4, y: 4, z: 8, core: 2. Of those that a mesh axis runs over, the one named last changes fastest.
Arguments:
- inputs: bfloat16 [4, 8192, 2048], P('stream', 'seq'), may hold values from -16 to 16
- cotangent: bfloat16 [4, 8192, 2048], P('stream', 'seq'), may hold values from -6 to 6
- lengths: int32 [4, 4], P('stream'), may hold values from 1 to 6144, 8192 in all within a row
- angles: float32 [2, 2048], replicated, may hold values from -3.140625 to 3.140625
- mix: float32 [14, 2048], replicated, may hold values from -1.5 to 1.5
- weight: bfloat16 [2048, 2048], replicated, may hold values from -0.125 to 0.125
Outputs:
- output: bfloat16 [4, 8192, 2048], P('stream', 'seq')
- input_grad: bfloat16 [4, 8192, 2048], P('stream', 'seq')
- weight_grad: float32 [2048, 2048], P('seq')
- angle_grad: float32 [2, 2048], replicated
- mix_grad: float32 [14, 2048], replicated
Inputs may be any that keep to these rules, and one draw needn't show every extreme that they name: Each row holds the lengths of the 4 documents of one stream in time order; they sum to 8192, and the longest is exactly 6144.
All inputs are finite; a program needn't handle non-finite values.
Results may differ from a plain program's by a relative error of at most 0.012.
Values may be sent and summed in bfloat16 or wider, within the bound.
No kernel may reach another device: no remote copies, remote signals or barrier semaphores. Data moves between devices by JAX's collectives and lax.ppermute only.
A program may use at most 128 MiB of HBM per device.

v0:
```python
import jax
import jax.numpy as jnp
from jax import lax
from jax.sharding import PartitionSpec as P


def from_behind(block, axis, distance):
    devices = range(lax.axis_size(axis))
    route = [(i - distance, i) for i in devices if i - distance in devices]
    return lax.ppermute(block, axis, route)


def segment_start(lengths_row, times):
    ends = jnp.cumsum(lengths_row, dtype=jnp.int32)
    hits = jnp.where(ends[None, :] <= times[:, None], lengths_row[None, :], 0)
    return jnp.sum(hits, axis=1, dtype=jnp.int32)


def tap_mask(times, start, dist):
    return (times - dist >= start).astype(jnp.float32)


def body(inputs, cotangent, lengths, angles, mix, weight):
    local_in = inputs[0]
    local_cot = cotangent[0]
    rows, width = local_in.shape
    seq_count = lax.axis_size("seq")
    stream_count = lax.axis_size("stream")
    far_count = seq_count.bit_length() - 1
    near_count = rows.bit_length() - 1
    levels = near_count + far_count
    total = rows * seq_count
    factor = float(stream_count * total) ** (-0.5)
    member = lax.axis_index("seq")
    cos_a = jnp.cos(angles[0])
    sin_a = jnp.sin(angles[0])
    cos_d = jnp.cos(angles[1])
    sin_d = jnp.sin(angles[1])
    times = member * rows + jnp.arange(rows, dtype=jnp.int32)
    start = segment_start(lengths[0], times)
    masks = [tap_mask(times, start, 2**level)[:, None] for level in range(levels)]
    current = local_in
    stored = [current]
    taps = []
    mixed = jnp.zeros((rows, width), jnp.float32)
    for level in range(near_count):
        dist = 2**level
        before = from_behind(current[rows - dist :], "seq", 1)
        shifted = (
            jnp.concatenate([before, current[: rows - dist]], axis=0).astype(jnp.float32)
            * masks[level]
        )
        plain = current.astype(jnp.float32)
        mixed = mixed + mix[level] * (cos_d * plain + sin_d * shifted)
        current = lax.optimization_barrier((cos_a * plain + sin_a * shifted).astype(jnp.bfloat16))
        taps.append(shifted.astype(jnp.bfloat16))
        stored.append(current)
    for level in range(near_count, levels):
        dist = 2**level
        arrived = from_behind(current, "seq", dist // rows)
        shifted = arrived.astype(jnp.float32) * masks[level]
        plain = current.astype(jnp.float32)
        mixed = mixed + mix[level] * (cos_d * plain + sin_d * shifted)
        current = lax.optimization_barrier((cos_a * plain + sin_a * shifted).astype(jnp.bfloat16))
        taps.append(shifted.astype(jnp.bfloat16))
        stored.append(current)
    mixed = mixed + mix[levels] * current.astype(jnp.float32)
    act = jax.nn.gelu(mixed).astype(jnp.bfloat16)
    output = jnp.dot(act, weight, preferred_element_type=jnp.float32).astype(jnp.bfloat16)
    act_grad = lax.optimization_barrier(
        lax.dot_general(
            local_cot, weight, (((1,), (1,)), ((), ())), preferred_element_type=jnp.float32
        ).astype(jnp.bfloat16)
    )
    unused, pull = jax.vjp(jax.nn.gelu, mixed)
    mixed_grad = lax.optimization_barrier(
        pull(act_grad.astype(jnp.float32))[0].astype(jnp.bfloat16)
    )
    grad_full = mixed_grad.astype(jnp.float32)
    upper = mix[levels] * grad_full
    mix_rows = [None] * (levels + 1)
    mix_rows[levels] = jnp.sum(grad_full * stored[levels].astype(jnp.float32), axis=0)
    theta = jnp.zeros((width,), jnp.float32)
    phi = jnp.zeros((width,), jnp.float32)
    carried = stored[0]
    for level in reversed(range(levels)):
        dist = 2**level
        plain = stored[level].astype(jnp.float32)
        shifted = taps[level].astype(jnp.float32)
        along = mix[level] * grad_full
        mix_rows[level] = jnp.sum(grad_full * (cos_d * plain + sin_d * shifted), axis=0)
        theta = theta + jnp.sum(upper * (cos_a * shifted - sin_a * plain), axis=0)
        phi = phi + jnp.sum(along * (cos_d * shifted - sin_d * plain), axis=0)
        sent = lax.optimization_barrier(
            (masks[level] * (sin_a * upper + sin_d * along)).astype(jnp.bfloat16)
        )
        if dist < rows:
            after = from_behind(sent[:dist], "seq", -1)
            back = jnp.concatenate([sent[dist:], after], axis=0)
        else:
            back = from_behind(sent, "seq", -(dist // rows))
        carried = lax.optimization_barrier(
            (cos_a * upper + cos_d * along + back.astype(jnp.float32)).astype(jnp.bfloat16)
        )
        upper = carried.astype(jnp.float32)
    angle_all, mix_all = lax.psum((jnp.stack([theta, phi]), jnp.stack(mix_rows)), ("stream", "seq"))
    weight_rows = lax.psum_scatter(
        lax.dot_general(
            act, local_cot, (((0,), (0,)), ((), ())), preferred_element_type=jnp.float32
        ),
        "seq",
        scatter_dimension=0,
        tiled=True,
    )
    weight_rows = lax.psum(weight_rows, "stream")
    return (output[None], carried[None], weight_rows * factor, angle_all * factor, mix_all * factor)


def solution(mesh):
    in_specs = (
        P("stream", "seq", None),
        P("stream", "seq", None),
        P("stream", None),
        P(),
        P(),
        P(),
    )
    out_specs = (P("stream", "seq", None), P("stream", "seq", None), P("seq", None), P(), P())
    return jax.shard_map(body, mesh=mesh, in_specs=in_specs, out_specs=out_specs, check_vma=False)
```

profile of v0, /device:TPU:8, one launch (start us, length us, event | category | flops | bytes accessed | tf_op | source)
XLA Modules:
  0.0 812.0 jit_solution(9908100230172136991)
XLA Ops:
  17.4 3.6 collective-permute-start.1
  25.5 3.1 collective-permute-done.2
  31.6 3.3 collective-permute-done.3
  35.9 2.1 collective-permute-start.4
  38.0 3.6 collective-permute-done.4
  44.5 4.3 collective-permute-done.5
  51.7 5.8 collective-permute-done.6
  58.5 2.1 collective-permute-start.7
  60.6 8.6 %collective-permute-done.7 = bf16[128,2048]{1,0:T(8,128)(2,1)S(1)} collective-permute-done((bf16[128,2048]{1,0:T(8,128)(2,1)S(1)}, bf16[128,2048]{1,0:T(8,128)(2,1)S(1)}, u32[]{:S(2)}, u32[]{:S(2)}) %collective-permute-start.7) | collective-permute-done | bytes 524320 | tf_op jit(solution)/shard_map/ppermute | solution.py:10
  70.1 3.5 collective-permute-start.8
  73.6 11.4 %collective-permute-done.8 = bf16[128,2048]{1,0:T(8,128)(2,1)S(1)} collective-permute-done((bf16[128,2048]{1,0:T(8,128)(2,1)S(1)}, bf16[128,2048]{1,0:T(8,128)(2,1)S(1)}, u32[]{:S(2)}, u32[]{:S(2)}) %collective-permute-start.8) | collective-permute-done | bytes 524320 | tf_op jit(solution)/shard_map/ppermute | solution.py:10
  86.0 15.0 %collective-permute-start.9 = (bf16[128,2048]{1,0:T(8,128)(2,1)S(1)}, bf16[128,2048]{1,0:T(8,128)(2,1)S(1)}, u32[]{:S(2)}, u32[]{:S(2)}) collective-permute-start(bf16[128,2048]{1,0:T(8,128)(2,1)S(1)} %fusion.250), channel_id=1, source_target_pairs={{0,4},{1,5},{2,6},{3,7},{4,8},{5,9},{6,10},{7,11},{8,12},{9,13},{1... | collective-permute-start | bytes 1572872 | tf_op jit(solution)/shard_map/ppermute | solution.py:10
  101.0 7.5 collective-permute-done.9
  109.4 4.3 collective-permute-start.10
  113.8 6.6 collective-permute-done.10
  121.4 14.6 %collective-permute-start.11 = (bf16[128,2048]{1,0:T(8,128)(2,1)S(1)}, bf16[128,2048]{1,0:T(8,128)(2,1)S(1)}, u32[]{:S(2)}, u32[]{:S(2)}) collective-permute-start(bf16[128,2048]{1,0:T(8,128)(2,1)S(1)} %fusion.254), channel_id=1, source_target_pairs={{0,16},{1,17},{2,18},{3,19},{4,20},{5,21},{6,22},{7,23},{8,24},{9,... | collective-permute-start | bytes 1572872 | tf_op jit(solution)/shard_map/ppermute | solution.py:10
  136.0 8.1 collective-permute-done.11
  145.0 31.3 %collective-permute-start.12 = (bf16[128,2048]{1,0:T(8,128)(2,1)S(1)}, bf16[128,2048]{1,0:T(8,128)(2,1)S(1)}, u32[]{:S(2)}, u32[]{:S(2)}) collective-permute-start(bf16[128,2048]{1,0:T(8,128)(2,1)S(1)} %fusion.256), channel_id=1, source_target_pairs={{0,32},{1,33},{2,34},{3,35},{4,36},{5,37},{6,38},{7,39},{8,40},{9,... | collective-permute-start | bytes 1572872 | tf_op jit(solution)/shard_map/ppermute | solution.py:10
  176.4 2.9 convolution_convert_fusion
  179.5 7.8 collective-permute-done.12
  188.4 7.4 fusion.97
  197.1 8.1 %fusion.288 = f32[2048,2048]{1,0:T(8,128)} fusion(bf16[1,128,2048]{2,1,0:T(8,128)(2,1)S(1)} %copy-done, f32[128,2048]{1,0:T(8,128)S(1)} %get-tuple-element.55), kind=kOutput, calls=%fused_computation.471 | convolution fusion | flops 1076101120 | bytes 18350080 | tf_op jit(solution)/shard_map/dot_general | solution.py:108
  208.0 19.3 %collective-permute-done.13 = bf16[128,2048]{1,0:T(8,128)(2,1)S(1)} collective-permute-done((bf16[128,2048]{1,0:T(8,128)(2,1)S(1)}, bf16[128,2048]{1,0:T(8,128)(2,1)S(1)}, u32[]{:S(2)}, u32[]{:S(2)}) %collective-permute-start.13) | collective-permute-done | bytes 524320 | tf_op jit(solution)/shard_map/ppermute | solution.py:10
  230.6 26.2 %collective-permute-done.14 = bf16[128,2048]{1,0:T(8,128)(2,1)S(1)} collective-permute-done((bf16[128,2048]{1,0:T(8,128)(2,1)S(1)}, bf16[128,2048]{1,0:T(8,128)(2,1)S(1)}, u32[]{:S(2)}, u32[]{:S(2)}) %collective-permute-start.14) | collective-permute-done | bytes 524320 | tf_op jit(solution)/shard_map/ppermute | solution.py:10
  260.5 13.7 %collective-permute-done.15 = bf16[128,2048]{1,0:T(8,128)(2,1)S(1)} collective-permute-done((bf16[128,2048]{1,0:T(8,128)(2,1)S(1)}, bf16[128,2048]{1,0:T(8,128)(2,1)S(1)}, u32[]{:S(2)}, u32[]{:S(2)}) %collective-permute-start.15) | collective-permute-done | bytes 524320 | tf_op jit(solution)/shard_map/ppermute | solution.py:10
  275.4 3.1 fusion.270
  279.7 19.8 %collective-permute-done.16 = bf16[128,2048]{1,0:T(8,128)(2,1)S(1)} collective-permute-done((bf16[128,2048]{1,0:T(8,128)(2,1)S(1)}, bf16[128,2048]{1,0:T(8,128)(2,1)S(1)}, u32[]{:S(2)}, u32[]{:S(2)}) %collective-permute-start.16) | collective-permute-done | bytes 524320 | tf_op jit(solution)/shard_map/ppermute | solution.py:10
  299.9 3.1 fusion.269
  303.0 10.8 %collective-permute-start.17 = (bf16[128,2048]{1,0:T(8,128)(2,1)S(1)}, bf16[128,2048]{1,0:T(8,128)(2,1)S(1)}, u32[]{:S(2)}, u32[]{:S(2)}) collective-permute-start(bf16[128,2048]{1,0:T(8,128)(2,1)S(1)} %get-tuple-element.57), channel_id=1, source_target_pairs={{2,0},{3,1},{4,2},{5,3},{6,4},{7,5},{8,6},{9,7},{10,8},{11,9},{12,... | collective-permute-start | bytes 1572872 | tf_op jit(solution)/shard_map/ppermute | solution.py:10
  313.9 22.7 %collective-permute-done.17 = bf16[128,2048]{1,0:T(8,128)(2,1)S(1)} collective-permute-done((bf16[128,2048]{1,0:T(8,128)(2,1)S(1)}, bf16[128,2048]{1,0:T(8,128)(2,1)S(1)}, u32[]{:S(2)}, u32[]{:S(2)}) %collective-permute-start.17) | collective-permute-done | bytes 524320 | tf_op jit(solution)/shard_map/ppermute | solution.py:10
  337.0 3.0 fusion.268
  341.9 6.7 collective-permute-done.18
  348.9 2.2 fusion.267
  351.2 4.2 collective-permute-start.19
  355.4 3.9 collective-permute-done.19
  359.6 2.2 fusion.266
  361.8 4.2 collective-permute-start.20
  366.1 5.5 collective-permute-done.20
  373.5 3.4 collective-permute-start.21
  376.9 5.1 collective-permute-done.21
  386.0 3.6 collective-permute-done.22
  393.8 3.1 collective-permute-done.23
  399.2 2.1 collective-permute-start.24
  401.3 2.3 fusion
  406.6 2.2 collective-permute-start.25
  408.9 101.6 %psum.22 = f32[2,2048]{1,0:T(2,128)S(1)} all-reduce(f32[2,2048]{1,0:T(2,128)S(1)} %pad_maximum_fusion.7), channel_id=1, replica_groups=mesh['stream'=4,'seq'=64] {'stream','seq'}, use_global_device_ids=true, to_apply=%region_30.31 | all-reduce | flops 4096 | bytes 32768 | tf_op jit(solution)/shard_map/psum | solution.py:106
  514.0 243.3 %all-reduce.5.cloned.1.call-done = f32[14,2048]{1,0:T(8,128)} async-done(((f32[14,2048]{1,0:T(8,128)}), f32[14,2048]{1,0:T(8,128)}) %all-reduce.5.cloned.1.call-update) | async-done | bytes 114704 | tf_op jit(solution)/shard_map/psum | solution.py:106
  758.8 43.9 %all-reduce.3.cloned.1.call-done = f32[32,2048]{1,0:T(8,128)} async-done(((f32[32,2048]{1,0:T(8,128)}), f32[32,2048]{1,0:T(8,128)}) %all-reduce.3.cloned.1.call-update) | async-done | bytes 262160 | tf_op jit(solution)/shard_map/psum | solution.py:115
  (302 shorter events, 68.1 us)
Async XLA Ops:
  8.0 168.4 %copy-start = (bf16[1,128,2048]{2,1,0:T(8,128)(2,1)S(1)}, bf16[1,128,2048]{2,1,0:T(8,128)(2,1)}, u32[]{:S(2)}) copy-start(bf16[1,128,2048]{2,1,0:T(8,128)(2,1)} %param.7) | copy-start | bytes 1572868
  8.0 505.9 %reduce-scatter.2.cloned.1.call-start = ((), (), s32[]{:S(2)}) async-start(), calls=%async_computation.1 | async-start | bytes 17039360 | tf_op jit(solution)/shard_map/reduce_scatter | solution.py:107
  8.9 7.1 collective-permute-start
  17.4 5.1 collective-permute-start.1
  23.6 5.1 collective-permute-start.2
  28.6 159.6 %copy-start.65 = (bf16[4,2048]{1,0:T(4,128)(2,1)}, bf16[4,2048]{1,0:T(4,128)(2,1)S(1)}, u32[]{:S(2)}) copy-start(bf16[4,2048]{1,0:T(4,128)(2,1)S(1)} %collective-permute-done.2) | copy-start | bytes 49156
  29.7 5.2 collective-permute-start.3
  31.6 156.6 %copy-start.22 = (bf16[120,2048]{1,0:T(8,128)(2,1)}, bf16[120,2048]{1,0:T(8,128)(2,1)S(1)}, u32[]{:S(2)}) copy-start(bf16[120,2048]{1,0:T(8,128)(2,1)S(1)} %slice.205) | copy-start | bytes 1474564
  34.9 153.4 %copy-start.55 = (bf16[8,2048]{1,0:T(8,128)(2,1)}, bf16[8,2048]{1,0:T(8,128)(2,1)S(1)}, u32[]{:S(2)}) copy-start(bf16[8,2048]{1,0:T(8,128)(2,1)S(1)} %collective-permute-done.3) | copy-start | bytes 98308
  34.9 141.5 %slice-start = ((s8[8388608]{0:T(1024)(128)(4,1)}), s8[4194304]{0:T(1024)(128)(4,1)S(1)}, s32[]{:S(2)}) async-start(s8[8388608]{0:T(1024)(128)(4,1)} %bitcast.103), calls=%async_computation.4 | async-start | bytes 8388608
  35.9 5.7 collective-permute-start.4
  38.0 150.2 %copy-start.24 = (bf16[112,2048]{1,0:T(8,128)(2,1)}, bf16[112,2048]{1,0:T(8,128)(2,1)S(1)}, u32[]{:S(2)}) copy-start(bf16[112,2048]{1,0:T(8,128)(2,1)S(1)} %slice.207) | copy-start | bytes 1376260
  41.7 146.6 %copy-start.53 = (bf16[16,2048]{1,0:T(8,128)(2,1)}, bf16[16,2048]{1,0:T(8,128)(2,1)S(1)}, u32[]{:S(2)}) copy-start(bf16[16,2048]{1,0:T(8,128)(2,1)S(1)} %collective-permute-done.4) | copy-start | bytes 196612
  42.5 145.8 %copy-start.1 = (bf16[128,2048]{1,0:T(8,128)(2,1)}, bf16[128,2048]{1,0:T(8,128)(2,1)S(1)}, u32[]{:S(2)}) copy-start(bf16[128,2048]{1,0:T(8,128)(2,1)S(1)} %fusion.242) | copy-start | bytes 1572868
  42.6 6.3 collective-permute-start.5
  48.8 139.5 %copy-start.51 = (bf16[32,2048]{1,0:T(8,128)(2,1)}, bf16[32,2048]{1,0:T(8,128)(2,1)S(1)}, u32[]{:S(2)}) copy-start(bf16[32,2048]{1,0:T(8,128)(2,1)S(1)} %collective-permute-done.5) | copy-start | bytes 393220
  49.7 138.6 %copy-start.3 = (bf16[128,2048]{1,0:T(8,128)(2,1)}, bf16[128,2048]{1,0:T(8,128)(2,1)S(1)}, u32[]{:S(2)}) copy-start(bf16[128,2048]{1,0:T(8,128)(2,1)S(1)} %fusion.244) | copy-start | bytes 1572868
  49.8 138.6 %copy-start.43 = (bf16[64,2048]{1,0:T(8,128)(2,1)}, bf16[64,2048]{1,0:T(8,128)(2,1)S(1)}, u32[]{:S(2)}) copy-start(bf16[64,2048]{1,0:T(8,128)(2,1)S(1)} %get-tuple-element.69) | copy-start | bytes 786436
  49.8 7.7 collective-permute-start.6
  57.5 130.9 %copy-start.47 = (bf16[64,2048]{1,0:T(8,128)(2,1)}, bf16[64,2048]{1,0:T(8,128)(2,1)S(1)}, u32[]{:S(2)}) copy-start(bf16[64,2048]{1,0:T(8,128)(2,1)S(1)} %collective-permute-done.6) | copy-start | bytes 786436
  57.5 118.9 %slice-start.1 = ((s8[8388608]{0:T(1024)(128)(4,1)}), s8[4194304]{0:T(1024)(128)(4,1)S(1)}, s32[]{:S(2)}) async-start(s8[8388608]{0:T(1024)(128)(4,1)} %bitcast.103), calls=%async_computation.5 | async-start | bytes 8388608
  58.5 129.9 %copy-start.18 = (bf16[128,2048]{1,0:T(8,128)(2,1)}, bf16[128,2048]{1,0:T(8,128)(2,1)S(1)}, u32[]{:S(2)}) copy-start(bf16[128,2048]{1,0:T(8,128)(2,1)S(1)} %fusion.246) | copy-start | bytes 1572868
  58.5 10.6 %collective-permute-start.7 = (bf16[128,2048]{1,0:T(8,128)(2,1)S(1)}, bf16[128,2048]{1,0:T(8,128)(2,1)S(1)}, u32[]{:S(2)}, u32[]{:S(2)}) collective-permute-start(bf16[128,2048]{1,0:T(8,128)(2,1)S(1)} %fusion.246), channel_id=1, source_target_pairs={{0,1},{1,2},{2,3},{3,4},{4,5},{5,6},{6,7},{7,8},{8,9},{9,10},{10,1... | collective-permute-start | bytes 1572872 | tf_op jit(solution)/shard_map/ppermute | solution.py:10
  69.1 119.2 %copy-start.39 = (bf16[128,2048]{1,0:T(8,128)(2,1)}, bf16[128,2048]{1,0:T(8,128)(2,1)S(1)}, u32[]{:S(2)}) copy-start(bf16[128,2048]{1,0:T(8,128)(2,1)S(1)} %collective-permute-done.7) | copy-start | bytes 1572868
  70.1 118.3 %copy-start.7 = (bf16[128,2048]{1,0:T(8,128)(2,1)}, bf16[128,2048]{1,0:T(8,128)(2,1)S(1)}, u32[]{:S(2)}) copy-start(bf16[128,2048]{1,0:T(8,128)(2,1)S(1)} %fusion.248) | copy-start | bytes 1572868
  70.1 14.9 %collective-permute-start.8 = (bf16[128,2048]{1,0:T(8,128)(2,1)S(1)}, bf16[128,2048]{1,0:T(8,128)(2,1)S(1)}, u32[]{:S(2)}, u32[]{:S(2)}) collective-permute-start(bf16[128,2048]{1,0:T(8,128)(2,1)S(1)} %fusion.248), channel_id=1, source_target_pairs={{0,2},{1,3},{2,4},{3,5},{4,6},{5,7},{6,8},{7,9},{8,10},{9,11},{10,... | collective-permute-start | bytes 1572872 | tf_op jit(solution)/shard_map/ppermute | solution.py:10
  86.0 22.5 %collective-permute-start.9 = (bf16[128,2048]{1,0:T(8,128)(2,1)S(1)}, bf16[128,2048]{1,0:T(8,128)(2,1)S(1)}, u32[]{:S(2)}, u32[]{:S(2)}) collective-permute-start(bf16[128,2048]{1,0:T(8,128)(2,1)S(1)} %fusion.250), channel_id=1, source_target_pairs={{0,4},{1,5},{2,6},{3,7},{4,8},{5,9},{6,10},{7,11},{8,12},{9,13},{1... | collective-permute-start | bytes 1572872 | tf_op jit(solution)/shard_map/ppermute | solution.py:10
  109.4 11.0 %collective-permute-start.10 = (bf16[128,2048]{1,0:T(8,128)(2,1)S(1)}, bf16[128,2048]{1,0:T(8,128)(2,1)S(1)}, u32[]{:S(2)}, u32[]{:S(2)}) collective-permute-start(bf16[128,2048]{1,0:T(8,128)(2,1)S(1)} %fusion.252), channel_id=1, source_target_pairs={{0,8},{1,9},{2,10},{3,11},{4,12},{5,13},{6,14},{7,15},{8,16},{9,17... | collective-permute-start | bytes 1572872 | tf_op jit(solution)/shard_map/ppermute | solution.py:10
  121.4 22.7 %collective-permute-start.11 = (bf16[128,2048]{1,0:T(8,128)(2,1)S(1)}, bf16[128,2048]{1,0:T(8,128)(2,1)S(1)}, u32[]{:S(2)}, u32[]{:S(2)}) collective-permute-start(bf16[128,2048]{1,0:T(8,128)(2,1)S(1)} %fusion.254), channel_id=1, source_target_pairs={{0,16},{1,17},{2,18},{3,19},{4,20},{5,21},{6,22},{7,23},{8,24},{9,... | collective-permute-start | bytes 1572872 | tf_op jit(solution)/shard_map/ppermute | solution.py:10
  145.0 42.4 %collective-permute-start.12 = (bf16[128,2048]{1,0:T(8,128)(2,1)S(1)}, bf16[128,2048]{1,0:T(8,128)(2,1)S(1)}, u32[]{:S(2)}, u32[]{:S(2)}) collective-permute-start(bf16[128,2048]{1,0:T(8,128)(2,1)S(1)} %fusion.256), channel_id=1, source_target_pairs={{0,32},{1,33},{2,34},{3,35},{4,36},{5,37},{6,38},{7,39},{8,40},{9,... | collective-permute-start | bytes 1572872 | tf_op jit(solution)/shard_map/ppermute | solution.py:10
  205.2 552.0 %all-reduce.5.cloned.1.call-start = ((), (), s32[]{:S(2)}) async-start(), calls=%async_computation.3 | async-start | bytes 262144 | tf_op jit(solution)/shard_map/psum | solution.py:106
  206.6 20.8 %collective-permute-start.13 = (bf16[128,2048]{1,0:T(8,128)(2,1)S(1)}, bf16[128,2048]{1,0:T(8,128)(2,1)S(1)}, u32[]{:S(2)}, u32[]{:S(2)}) collective-permute-start(bf16[128,2048]{1,0:T(8,128)(2,1)S(1)} %fusion.189), channel_id=1, source_target_pairs={{32,0},{33,1},{34,2},{35,3},{36,4},{37,5},{38,6},{39,7},{40,8},{41... | collective-permute-start | bytes 1572872 | tf_op jit(solution)/shard_map/ppermute | solution.py:10
  229.3 27.5 %collective-permute-start.14 = (bf16[128,2048]{1,0:T(8,128)(2,1)S(1)}, bf16[128,2048]{1,0:T(8,128)(2,1)S(1)}, u32[]{:S(2)}, u32[]{:S(2)}) collective-permute-start(bf16[128,2048]{1,0:T(8,128)(2,1)S(1)} %fusion.182), channel_id=1, source_target_pairs={{16,0},{17,1},{18,2},{19,3},{20,4},{21,5},{22,6},{23,7},{24,8},{25... | collective-permute-start | bytes 1572872 | tf_op jit(solution)/shard_map/ppermute | solution.py:10
  259.1 15.1 %collective-permute-start.15 = (bf16[128,2048]{1,0:T(8,128)(2,1)S(1)}, bf16[128,2048]{1,0:T(8,128)(2,1)S(1)}, u32[]{:S(2)}, u32[]{:S(2)}) collective-permute-start(bf16[128,2048]{1,0:T(8,128)(2,1)S(1)} %fusion.175), channel_id=1, source_target_pairs={{8,0},{9,1},{10,2},{11,3},{12,4},{13,5},{14,6},{15,7},{16,8},{17,9... | collective-permute-start | bytes 1572872 | tf_op jit(solution)/shard_map/ppermute | solution.py:10
  278.5 21.1 %collective-permute-start.16 = (bf16[128,2048]{1,0:T(8,128)(2,1)S(1)}, bf16[128,2048]{1,0:T(8,128)(2,1)S(1)}, u32[]{:S(2)}, u32[]{:S(2)}) collective-permute-start(bf16[128,2048]{1,0:T(8,128)(2,1)S(1)} %get-tuple-element.56), channel_id=1, source_target_pairs={{4,0},{5,1},{6,2},{7,3},{8,4},{9,5},{10,6},{11,7},{12,8},{13,9},{1... | collective-permute-start | bytes 1572872 | tf_op jit(solution)/shard_map/ppermute | solution.py:10
  303.0 33.5 %collective-permute-start.17 = (bf16[128,2048]{1,0:T(8,128)(2,1)S(1)}, bf16[128,2048]{1,0:T(8,128)(2,1)S(1)}, u32[]{:S(2)}, u32[]{:S(2)}) collective-permute-start(bf16[128,2048]{1,0:T(8,128)(2,1)S(1)} %get-tuple-element.57), channel_id=1, source_target_pairs={{2,0},{3,1},{4,2},{5,3},{6,4},{7,5},{8,6},{9,7},{10,8},{11,9},{12,... | collective-permute-start | bytes 1572872 | tf_op jit(solution)/shard_map/ppermute | solution.py:10
  340.0 8.6 %collective-permute-start.18 = (bf16[128,2048]{1,0:T(8,128)(2,1)S(1)}, bf16[128,2048]{1,0:T(8,128)(2,1)S(1)}, u32[]{:S(2)}, u32[]{:S(2)}) collective-permute-start(bf16[128,2048]{1,0:T(8,128)(2,1)S(1)} %get-tuple-element.58), channel_id=1, source_target_pairs={{1,0},{2,1},{3,2},{4,3},{5,4},{6,5},{7,6},{8,7},{9,8},{10,9},{11,1... | collective-permute-start | bytes 1572872 | tf_op jit(solution)/shard_map/ppermute | solution.py:10
  351.2 8.1 collective-permute-start.19
  361.8 9.7 %collective-permute-start.20 = (bf16[32,2048]{1,0:T(8,128)(2,1)S(1)}, bf16[32,2048]{1,0:T(8,128)(2,1)S(1)}, u32[]{:S(2)}, u32[]{:S(2)}) collective-permute-start(bf16[32,2048]{1,0:T(8,128)(2,1)S(1)} %slice.215), channel_id=1, source_target_pairs={{1,0},{2,1},{3,2},{4,3},{5,4},{6,5},{7,6},{8,7},{9,8},{10,9},{11,1... | collective-permute-start | bytes 393224 | tf_op jit(solution)/shard_map/ppermute | solution.py:10
  373.5 8.6 %collective-permute-start.21 = (bf16[16,2048]{1,0:T(8,128)(2,1)S(1)}, bf16[16,2048]{1,0:T(8,128)(2,1)S(1)}, u32[]{:S(2)}, u32[]{:S(2)}) collective-permute-start(bf16[16,2048]{1,0:T(8,128)(2,1)S(1)} %slice.217), channel_id=1, source_target_pairs={{1,0},{2,1},{3,2},{4,3},{5,4},{6,5},{7,6},{8,7},{9,8},{10,9},{11,1... | collective-permute-start | bytes 196616 | tf_op jit(solution)/shard_map/ppermute | solution.py:10
  384.0 5.5 collective-permute-start.22
  391.8 5.2 collective-permute-start.23
  399.1 112.1 %copy-start.91 = (f32[2048]{0:T(1024)S(1)}, f32[2048]{0:T(1024)}, u32[]{:S(2)}) copy-start(f32[2048]{0:T(1024)} %get-tuple-element.17) | copy-start | bytes 24580
  399.2 112.1 %copy-start.92 = (f32[2048]{0:T(1024)S(1)}, f32[2048]{0:T(1024)}, u32[]{:S(2)}) copy-start(f32[2048]{0:T(1024)} %get-tuple-element.52) | copy-start | bytes 24580
  399.2 113.6 %copy-start.28 = (f32[1,2048]{1,0:T(1,128)S(1)}, f32[1,2048]{1,0:T(1,128)}, u32[]{:S(2)}) copy-start(f32[1,2048]{1,0:T(1,128)} %get-tuple-element.84) | copy-start | bytes 24580
  399.2 5.2 collective-permute-start.24
  406.6 106.2 %collective-permute-start.25 = (bf16[1,2048]{1,0:T(2,128)(2,1)S(1)}, bf16[1,2048]{1,0:T(2,128)(2,1)S(1)}, u32[]{:S(2)}, u32[]{:S(2)}) collective-permute-start(bf16[1,2048]{1,0:T(2,128)(2,1)S(1)} %slice.225), channel_id=1, source_target_pairs={{1,0},{2,1},{3,2},{4,3},{5,4},{6,5},{7,6},{8,7},{9,8},{10,9},{11,1... | collective-permute-start | bytes 12296 | tf_op jit(solution)/shard_map/ppermute | solution.py:10
  512.7 289.9 %all-reduce.3.cloned.1.call-start = ((), (), s32[]{:S(2)}) async-start(), calls=%async_computation.2 | async-start | bytes 524288 | tf_op jit(solution)/shard_map/psum | solution.py:115
  (84 other events, 4780.8 us)
Sparse Core Ops, SparseCore 0:
  205.4 223.6 reduce-scatter.1
Sparse Core Ops, SparseCore 1:
  512.8 244.4 all-reduce.4
  759.4 43.2 all-reduce.2
where the time goes:
time: 819 us; the launch traced here: 812 us
  waiting for transfers between devices  489 us (60%)
  starting transfers between devices  124 us (15%)
  blocking collectives  102 us (12%)
  other arithmetic  58.4 us (7%)
  between operations  17.8 us (2%)
  matrix products  13.3 us (2%)
    psum x1, waiting for transfers between devices, body(): lax.psum((jnp.stack([theta, phi]), jnp.stack(mix_rows)), ('stream', 'seq'))  243 us
    ppermute x26, waiting for transfers between devices, from_behind(): return lax.ppermute(block, axis, route)  202 us
    ppermute x26, starting transfers between devices, from_behind(): return lax.ppermute(block, axis, route)  124 us
    psum x1, blocking collectives, body(): lax.psum((jnp.stack([theta, phi]), jnp.stack(mix_rows)), ('stream', 'seq'))  102 us
    psum x1, waiting for transfers between devices, body(): weight_rows = lax.psum(weight_rows, 'stream')  43.9 us
    reduce_sum x10, other arithmetic, body(): jnp.sum(grad_full * (cos_d * plain + sin_d * shifted), axis=0)  22.1 us
  transfers between devices with their start and end apart: 29, of which 26 were waited for; matrix products, arithmetic and copies ran while one was open for 6% of the time, Pallas kernels for 0%

commit v1 on v0

--- a/solution.py
+++ b/solution.py
@@ -112,7 +112,7 @@
         scatter_dimension=0,
         tiled=True,
     )
-    weight_rows = lax.psum(weight_rows, "stream")
+    weight_rows = jnp.sum(lax.all_gather(weight_rows, "stream"), axis=0)
     return (output[None], carried[None], weight_rows * factor, angle_all * factor, mix_all * factor)
 
 

time: 819 us -> 701 us (0.86)
  waiting for transfers between devices: 489 us -> 389 us
  blocking collectives: 102 us -> 83.9 us
    psum x1, waiting for transfers between devices: 243 us -> 168 us  [body(): lax.psum((jnp.stack([theta, phi]), jnp.stack(mix_rows)), ('stream', 'seq'))]
    psum x1 -> x0, waiting for transfers between devices: 43.9 us -> none  [body(): weight_rows = lax.psum(weight_rows, 'stream')]
    reduce_scatter x1, waiting for transfers between devices: 0.01 us -> 18.9 us  [body(): lax.psum_scatter(lax.dot_general(act, local_cot, (((0,), (0,)), ((), ()))...]
    psum x1, blocking collectives: 102 us -> 83.9 us  [body(): lax.psum((jnp.stack([theta, phi]), jnp.stack(mix_rows)), ('stream', 'seq'))]
  transfers between devices with their start and end apart: 29 -> 29, of which waited for: 26 -> 26; matrix products, arithmetic and copies ran while one was open for 6% -> 7% of each run, Pallas kernels for 0% -> 0%
where the time goes in v1:
time: 701 us; the launch traced here: 695 us
  waiting for transfers between devices  389 us (55%)
  starting transfers between devices  124 us (18%)
  blocking collectives  83.9 us (12%)
  other arithmetic  58.9 us (8%)
  between operations  18.1 us (3%)
  matrix products  13.4 us (2%)
  local copies, waits for them, and re-layouts  7.5 us (1%)
    ppermute x26, waiting for transfers between devices, from_behind(): return lax.ppermute(block, axis, route)  201 us
    psum x1, waiting for transfers between devices, body(): lax.psum((jnp.stack([theta, phi]), jnp.stack(mix_rows)), ('stream', 'seq'))  168 us
    ppermute x26, starting transfers between devices, from_behind(): return lax.ppermute(block, axis, route)  124 us
    psum x1, blocking collectives, body(): lax.psum((jnp.stack([theta, phi]), jnp.stack(mix_rows)), ('stream', 'seq'))  83.9 us
    reduce_sum x10, other arithmetic, body(): jnp.sum(grad_full * (cos_d * plain + sin_d * shifted), axis=0)  22.3 us
    reduce_scatter x1, waiting for transfers between devices, body(): lax.psum_scatter(lax.dot_general(act, local_cot, (((0,), (0,)), ((), ()))...  18.9 us
  transfers between devices with their start and end apart: 29, of which 26 were waited for; matrix products, arithmetic and copies ran while one was open for 7% of the time, Pallas kernels for 0%

profile of v1, /device:TPU:8, one launch (start us, length us, event | category | flops | bytes accessed | tf_op | source)
XLA Modules:
  0.0 694.6 jit_solution(1018018424241193688)
XLA Ops:
  8.9 1.9 collective-permute-start
  17.4 3.6 collective-permute-start.1
  25.5 3.1 collective-permute-done.2
  31.5 3.3 collective-permute-done.3
  35.9 2.1 collective-permute-start.4
  38.0 3.6 collective-permute-done.4
  44.6 4.3 collective-permute-done.5
  51.8 5.8 collective-permute-done.6
  58.6 2.1 collective-permute-start.7
  60.6 8.6 %collective-permute-done.7 = bf16[128,2048]{1,0:T(8,128)(2,1)S(1)} collective-permute-done((bf16[128,2048]{1,0:T(8,128)(2,1)S(1)}, bf16[128,2048]{1,0:T(8,128)(2,1)S(1)}, u32[]{:S(2)}, u32[]{:S(2)}) %collective-permute-start.7) | collective-permute-done | bytes 524320 | tf_op jit(solution)/shard_map/ppermute | solution.py:10
  70.2 3.5 collective-permute-start.8
  73.7 11.4 %collective-permute-done.8 = bf16[128,2048]{1,0:T(8,128)(2,1)S(1)} collective-permute-done((bf16[128,2048]{1,0:T(8,128)(2,1)S(1)}, bf16[128,2048]{1,0:T(8,128)(2,1)S(1)}, u32[]{:S(2)}, u32[]{:S(2)}) %collective-permute-start.8) | collective-permute-done | bytes 524320 | tf_op jit(solution)/shard_map/ppermute | solution.py:10
  86.0 15.1 %collective-permute-start.9 = (bf16[128,2048]{1,0:T(8,128)(2,1)S(1)}, bf16[128,2048]{1,0:T(8,128)(2,1)S(1)}, u32[]{:S(2)}, u32[]{:S(2)}) collective-permute-start(bf16[128,2048]{1,0:T(8,128)(2,1)S(1)} %fusion.250), channel_id=1, source_target_pairs={{0,4},{1,5},{2,6},{3,7},{4,8},{5,9},{6,10},{7,11},{8,12},{9,13},{1... | collective-permute-start | bytes 1572872 | tf_op jit(solution)/shard_map/ppermute | solution.py:10
  101.1 7.4 %collective-permute-done.9 = bf16[128,2048]{1,0:T(8,128)(2,1)S(1)} collective-permute-done((bf16[128,2048]{1,0:T(8,128)(2,1)S(1)}, bf16[128,2048]{1,0:T(8,128)(2,1)S(1)}, u32[]{:S(2)}, u32[]{:S(2)}) %collective-permute-start.9) | collective-permute-done | bytes 524320 | tf_op jit(solution)/shard_map/ppermute | solution.py:10
  109.5 4.4 collective-permute-start.10
  113.9 6.6 collective-permute-done.10
  121.5 14.6 %collective-permute-start.11 = (bf16[128,2048]{1,0:T(8,128)(2,1)S(1)}, bf16[128,2048]{1,0:T(8,128)(2,1)S(1)}, u32[]{:S(2)}, u32[]{:S(2)}) collective-permute-start(bf16[128,2048]{1,0:T(8,128)(2,1)S(1)} %fusion.254), channel_id=1, source_target_pairs={{0,16},{1,17},{2,18},{3,19},{4,20},{5,21},{6,22},{7,23},{8,24},{9,... | collective-permute-start | bytes 1572872 | tf_op jit(solution)/shard_map/ppermute | solution.py:10
  136.0 8.1 %collective-permute-done.11 = bf16[128,2048]{1,0:T(8,128)(2,1)S(1)} collective-permute-done((bf16[128,2048]{1,0:T(8,128)(2,1)S(1)}, bf16[128,2048]{1,0:T(8,128)(2,1)S(1)}, u32[]{:S(2)}, u32[]{:S(2)}) %collective-permute-start.11) | collective-permute-done | bytes 524320 | tf_op jit(solution)/shard_map/ppermute | solution.py:10
  145.0 31.3 %collective-permute-start.12 = (bf16[128,2048]{1,0:T(8,128)(2,1)S(1)}, bf16[128,2048]{1,0:T(8,128)(2,1)S(1)}, u32[]{:S(2)}, u32[]{:S(2)}) collective-permute-start(bf16[128,2048]{1,0:T(8,128)(2,1)S(1)} %fusion.256), channel_id=1, source_target_pairs={{0,32},{1,33},{2,34},{3,35},{4,36},{5,37},{6,38},{7,39},{8,40},{9,... | collective-permute-start | bytes 1572872 | tf_op jit(solution)/shard_map/ppermute | solution.py:10
  176.4 2.9 convolution_convert_fusion
  179.6 7.8 %collective-permute-done.12 = bf16[128,2048]{1,0:T(8,128)(2,1)S(1)} collective-permute-done((bf16[128,2048]{1,0:T(8,128)(2,1)S(1)}, bf16[128,2048]{1,0:T(8,128)(2,1)S(1)}, u32[]{:S(2)}, u32[]{:S(2)}) %collective-permute-start.12) | collective-permute-done | bytes 524320 | tf_op jit(solution)/shard_map/ppermute | solution.py:10
  188.4 7.4 %fusion.97 = (bf16[128,2048]{1,0:T(8,128)(2,1)S(1)}, f32[128,2048]{1,0:T(8,128)S(1)}) fusion(bf16[128,2048]{1,0:T(8,128)(2,1)S(1)} %convolution_convert_fusion, bf16[128,2048]{1,0:T(8,128)(2,1)S(1)} %fusion.258, f32[2048]{0:T(1024)S(1)} %bitcast.174, f32[128]{0:T(128)} %get-tuple-element.88, bf16[128,2048]{1,0:T(8,128)(2,1)S(1)} %collective-permute-done.12, ...), kind=kLoop, calls=%fused_computation.259 | loop fusion | flops 38797312 | bytes 16390656 | tf_op jit(solution)/shard_map/convert_element_type | solution.py:77
  197.0 8.2 %fusion.288 = f32[2048,2048]{1,0:T(8,128)} fusion(bf16[1,128,2048]{2,1,0:T(8,128)(2,1)S(1)} %copy-done, f32[128,2048]{1,0:T(8,128)S(1)} %get-tuple-element.55), kind=kOutput, calls=%fused_computation.471 | convolution fusion | flops 1076101120 | bytes 18350080 | tf_op jit(solution)/shard_map/dot_general | solution.py:108
  208.0 19.3 %collective-permute-done.13 = bf16[128,2048]{1,0:T(8,128)(2,1)S(1)} collective-permute-done((bf16[128,2048]{1,0:T(8,128)(2,1)S(1)}, bf16[128,2048]{1,0:T(8,128)(2,1)S(1)}, u32[]{:S(2)}, u32[]{:S(2)}) %collective-permute-start.13) | collective-permute-done | bytes 524320 | tf_op jit(solution)/shard_map/ppermute | solution.py:10
  230.6 26.2 %collective-permute-done.14 = bf16[128,2048]{1,0:T(8,128)(2,1)S(1)} collective-permute-done((bf16[128,2048]{1,0:T(8,128)(2,1)S(1)}, bf16[128,2048]{1,0:T(8,128)(2,1)S(1)}, u32[]{:S(2)}, u32[]{:S(2)}) %collective-permute-start.14) | collective-permute-done | bytes 524320 | tf_op jit(solution)/shard_map/ppermute | solution.py:10
  260.5 13.7 %collective-permute-done.15 = bf16[128,2048]{1,0:T(8,128)(2,1)S(1)} collective-permute-done((bf16[128,2048]{1,0:T(8,128)(2,1)S(1)}, bf16[128,2048]{1,0:T(8,128)(2,1)S(1)}, u32[]{:S(2)}, u32[]{:S(2)}) %collective-permute-start.15) | collective-permute-done | bytes 524320 | tf_op jit(solution)/shard_map/ppermute | solution.py:10
  275.3 3.1 fusion.270
  279.7 19.8 %collective-permute-done.16 = bf16[128,2048]{1,0:T(8,128)(2,1)S(1)} collective-permute-done((bf16[128,2048]{1,0:T(8,128)(2,1)S(1)}, bf16[128,2048]{1,0:T(8,128)(2,1)S(1)}, u32[]{:S(2)}, u32[]{:S(2)}) %collective-permute-start.16) | collective-permute-done | bytes 524320 | tf_op jit(solution)/shard_map/ppermute | solution.py:10
  299.9 3.0 fusion.269
  303.0 10.8 %collective-permute-start.17 = (bf16[128,2048]{1,0:T(8,128)(2,1)S(1)}, bf16[128,2048]{1,0:T(8,128)(2,1)S(1)}, u32[]{:S(2)}, u32[]{:S(2)}) collective-permute-start(bf16[128,2048]{1,0:T(8,128)(2,1)S(1)} %get-tuple-element.57), channel_id=1, source_target_pairs={{2,0},{3,1},{4,2},{5,3},{6,4},{7,5},{8,6},{9,7},{10,8},{11,9},{12,... | collective-permute-start | bytes 1572872 | tf_op jit(solution)/shard_map/ppermute | solution.py:10
  313.8 22.7 %collective-permute-done.17 = bf16[128,2048]{1,0:T(8,128)(2,1)S(1)} collective-permute-done((bf16[128,2048]{1,0:T(8,128)(2,1)S(1)}, bf16[128,2048]{1,0:T(8,128)(2,1)S(1)}, u32[]{:S(2)}, u32[]{:S(2)}) %collective-permute-start.17) | collective-permute-done | bytes 524320 | tf_op jit(solution)/shard_map/ppermute | solution.py:10
  336.9 3.0 fusion.268
  341.9 6.7 collective-permute-done.18
  348.9 2.2 fusion.267
  351.2 4.2 collective-permute-start.19
  355.4 3.9 collective-permute-done.19
  359.6 2.2 fusion.266
  361.8 4.2 collective-permute-start.20
  366.1 4.7 collective-permute-done.20
  372.8 3.4 collective-permute-start.21
  376.3 4.7 collective-permute-done.21
  384.9 3.6 collective-permute-done.22
  392.7 3.1 collective-permute-done.23
  398.2 2.1 collective-permute-start.24
  400.3 2.3 fusion
  410.1 18.9 %reduce-scatter.2.cloned.1.call-done = f32[32,2048]{1,0:T(8,128)} async-done(((f32[2048,2048]{1,0:T(8,128)}), f32[32,2048]{1,0:T(8,128)}) %reduce-scatter.2.cloned.1.call-update) | async-done | bytes 262160 | tf_op jit(solution)/shard_map/reduce_scatter | solution.py:107
  429.0 83.9 %psum.14 = f32[2,2048]{1,0:T(2,128)S(1)} all-reduce(f32[2,2048]{1,0:T(2,128)S(1)} %pad_maximum_fusion.7), channel_id=1, replica_groups=mesh['stream'=4,'seq'=64] {'stream','seq'}, use_global_device_ids=true, to_apply=%region_30.31 | all-reduce | flops 4096 | bytes 32768 | tf_op jit(solution)/shard_map/psum | solution.py:106
  514.8 168.4 %all-reduce.2.cloned.1.call-done = f32[14,2048]{1,0:T(8,128)} async-done(((f32[14,2048]{1,0:T(8,128)}), f32[14,2048]{1,0:T(8,128)}) %all-reduce.2.cloned.1.call-update) | async-done | bytes 114704 | tf_op jit(solution)/shard_map/psum | solution.py:106
  (335 shorter events, 69.2 us)
Async XLA Ops:
  8.0 168.3 %copy-start = (bf16[1,128,2048]{2,1,0:T(8,128)(2,1)S(1)}, bf16[1,128,2048]{2,1,0:T(8,128)(2,1)}, u32[]{:S(2)}) copy-start(bf16[1,128,2048]{2,1,0:T(8,128)(2,1)} %param.7) | copy-start | bytes 1572868
  8.0 421.0 %reduce-scatter.2.cloned.1.call-start = ((), (), s32[]{:S(2)}) async-start(), calls=%async_computation.1 | async-start | bytes 17039360 | tf_op jit(solution)/shard_map/reduce_scatter | solution.py:107
  8.9 7.1 %collective-permute-start = (bf16[1,2048]{1,0:T(2,128)(2,1)S(1)}, bf16[1,2048]{1,0:T(2,128)(2,1)S(1)}, u32[]{:S(2)}, u32[]{:S(2)}) collective-permute-start(bf16[1,2048]{1,0:T(2,128)(2,1)S(1)} %slice_bitcast_fusion.1), channel_id=1, source_target_pairs={{0,1},{1,2},{2,3},{3,4},{4,5},{5,6},{6,7},{7,8},{8,9},{9,10},{10,1... | collective-permute-start | bytes 12296 | tf_op jit(solution)/shard_map/ppermute | solution.py:10
  17.4 5.1 collective-permute-start.1
  23.5 5.1 collective-permute-start.2
  28.6 159.6 %copy-start.65 = (bf16[4,2048]{1,0:T(4,128)(2,1)}, bf16[4,2048]{1,0:T(4,128)(2,1)S(1)}, u32[]{:S(2)}) copy-start(bf16[4,2048]{1,0:T(4,128)(2,1)S(1)} %collective-permute-done.2) | copy-start | bytes 49156
  29.6 5.2 collective-permute-start.3
  31.5 156.7 %copy-start.22 = (bf16[120,2048]{1,0:T(8,128)(2,1)}, bf16[120,2048]{1,0:T(8,128)(2,1)S(1)}, u32[]{:S(2)}) copy-start(bf16[120,2048]{1,0:T(8,128)(2,1)S(1)} %slice.205) | copy-start | bytes 1474564
  34.8 153.5 %copy-start.55 = (bf16[8,2048]{1,0:T(8,128)(2,1)}, bf16[8,2048]{1,0:T(8,128)(2,1)S(1)}, u32[]{:S(2)}) copy-start(bf16[8,2048]{1,0:T(8,128)(2,1)S(1)} %collective-permute-done.3) | copy-start | bytes 98308
  34.8 141.6 %slice-start = ((s8[8388608]{0:T(1024)(128)(4,1)}), s8[4194304]{0:T(1024)(128)(4,1)S(1)}, s32[]{:S(2)}) async-start(s8[8388608]{0:T(1024)(128)(4,1)} %bitcast.104), calls=%async_computation.4 | async-start | bytes 8388608
  35.9 5.7 collective-permute-start.4
  38.0 150.3 %copy-start.24 = (bf16[112,2048]{1,0:T(8,128)(2,1)}, bf16[112,2048]{1,0:T(8,128)(2,1)S(1)}, u32[]{:S(2)}) copy-start(bf16[112,2048]{1,0:T(8,128)(2,1)S(1)} %slice.207) | copy-start | bytes 1376260
  41.6 146.6 %copy-start.53 = (bf16[16,2048]{1,0:T(8,128)(2,1)}, bf16[16,2048]{1,0:T(8,128)(2,1)S(1)}, u32[]{:S(2)}) copy-start(bf16[16,2048]{1,0:T(8,128)(2,1)S(1)} %collective-permute-done.4) | copy-start | bytes 196612
  42.6 145.7 %copy-start.1 = (bf16[128,2048]{1,0:T(8,128)(2,1)}, bf16[128,2048]{1,0:T(8,128)(2,1)S(1)}, u32[]{:S(2)}) copy-start(bf16[128,2048]{1,0:T(8,128)(2,1)S(1)} %fusion.242) | copy-start | bytes 1572868
  42.6 6.3 collective-permute-start.5
  48.9 139.4 %copy-start.51 = (bf16[32,2048]{1,0:T(8,128)(2,1)}, bf16[32,2048]{1,0:T(8,128)(2,1)S(1)}, u32[]{:S(2)}) copy-start(bf16[32,2048]{1,0:T(8,128)(2,1)S(1)} %collective-permute-done.5) | copy-start | bytes 393220
  49.8 138.5 %copy-start.3 = (bf16[128,2048]{1,0:T(8,128)(2,1)}, bf16[128,2048]{1,0:T(8,128)(2,1)S(1)}, u32[]{:S(2)}) copy-start(bf16[128,2048]{1,0:T(8,128)(2,1)S(1)} %fusion.244) | copy-start | bytes 1572868
  49.8 138.5 %copy-start.43 = (bf16[64,2048]{1,0:T(8,128)(2,1)}, bf16[64,2048]{1,0:T(8,128)(2,1)S(1)}, u32[]{:S(2)}) copy-start(bf16[64,2048]{1,0:T(8,128)(2,1)S(1)} %get-tuple-element.69) | copy-start | bytes 786436
  49.8 7.7 %collective-permute-start.6 = (bf16[64,2048]{1,0:T(8,128)(2,1)S(1)}, bf16[64,2048]{1,0:T(8,128)(2,1)S(1)}, u32[]{:S(2)}, u32[]{:S(2)}) collective-permute-start(bf16[64,2048]{1,0:T(8,128)(2,1)S(1)} %get-tuple-element.68), channel_id=1, source_target_pairs={{0,1},{1,2},{2,3},{3,4},{4,5},{5,6},{6,7},{7,8},{8,9},{9,10},{10,1... | collective-permute-start | bytes 786440 | tf_op jit(solution)/shard_map/ppermute | solution.py:10
  57.5 130.8 %copy-start.47 = (bf16[64,2048]{1,0:T(8,128)(2,1)}, bf16[64,2048]{1,0:T(8,128)(2,1)S(1)}, u32[]{:S(2)}) copy-start(bf16[64,2048]{1,0:T(8,128)(2,1)S(1)} %collective-permute-done.6) | copy-start | bytes 786436
  57.5 118.8 %slice-start.1 = ((s8[8388608]{0:T(1024)(128)(4,1)}), s8[4194304]{0:T(1024)(128)(4,1)S(1)}, s32[]{:S(2)}) async-start(s8[8388608]{0:T(1024)(128)(4,1)} %bitcast.104), calls=%async_computation.5 | async-start | bytes 8388608
  58.6 129.8 %copy-start.18 = (bf16[128,2048]{1,0:T(8,128)(2,1)}, bf16[128,2048]{1,0:T(8,128)(2,1)S(1)}, u32[]{:S(2)}) copy-start(bf16[128,2048]{1,0:T(8,128)(2,1)S(1)} %fusion.246) | copy-start | bytes 1572868
  58.6 10.6 %collective-permute-start.7 = (bf16[128,2048]{1,0:T(8,128)(2,1)S(1)}, bf16[128,2048]{1,0:T(8,128)(2,1)S(1)}, u32[]{:S(2)}, u32[]{:S(2)}) collective-permute-start(bf16[128,2048]{1,0:T(8,128)(2,1)S(1)} %fusion.246), channel_id=1, source_target_pairs={{0,1},{1,2},{2,3},{3,4},{4,5},{5,6},{6,7},{7,8},{8,9},{9,10},{10,1... | collective-permute-start | bytes 1572872 | tf_op jit(solution)/shard_map/ppermute | solution.py:10
  69.2 119.1 %copy-start.39 = (bf16[128,2048]{1,0:T(8,128)(2,1)}, bf16[128,2048]{1,0:T(8,128)(2,1)S(1)}, u32[]{:S(2)}) copy-start(bf16[128,2048]{1,0:T(8,128)(2,1)S(1)} %collective-permute-done.7) | copy-start | bytes 1572868
  69.2 110.1 %copy-start.87 = (f32[14,2048]{1,0:T(8,128)S(1)}, f32[14,2048]{1,0:T(8,128)}, u32[]{:S(2)}) copy-start(f32[14,2048]{1,0:T(8,128)} %param.10) | copy-start | bytes 344068
  70.2 118.2 %copy-start.7 = (bf16[128,2048]{1,0:T(8,128)(2,1)}, bf16[128,2048]{1,0:T(8,128)(2,1)S(1)}, u32[]{:S(2)}) copy-start(bf16[128,2048]{1,0:T(8,128)(2,1)S(1)} %fusion.248) | copy-start | bytes 1572868
  70.2 14.9 %collective-permute-start.8 = (bf16[128,2048]{1,0:T(8,128)(2,1)S(1)}, bf16[128,2048]{1,0:T(8,128)(2,1)S(1)}, u32[]{:S(2)}, u32[]{:S(2)}) collective-permute-start(bf16[128,2048]{1,0:T(8,128)(2,1)S(1)} %fusion.248), channel_id=1, source_target_pairs={{0,2},{1,3},{2,4},{3,5},{4,6},{5,7},{6,8},{7,9},{8,10},{9,11},{10,... | collective-permute-start | bytes 1572872 | tf_op jit(solution)/shard_map/ppermute | solution.py:10
  85.9 109.9 %copy-start.11 = (bf16[128,2048]{1,0:T(8,128)(2,1)}, bf16[128,2048]{1,0:T(8,128)(2,1)S(1)}, u32[]{:S(2)}) copy-start(bf16[128,2048]{1,0:T(8,128)(2,1)S(1)} %fusion.250) | copy-start | bytes 1572868
  86.0 22.5 %collective-permute-start.9 = (bf16[128,2048]{1,0:T(8,128)(2,1)S(1)}, bf16[128,2048]{1,0:T(8,128)(2,1)S(1)}, u32[]{:S(2)}, u32[]{:S(2)}) collective-permute-start(bf16[128,2048]{1,0:T(8,128)(2,1)S(1)} %fusion.250), channel_id=1, source_target_pairs={{0,4},{1,5},{2,6},{3,7},{4,8},{5,9},{6,10},{7,11},{8,12},{9,13},{1... | collective-permute-start | bytes 1572872 | tf_op jit(solution)/shard_map/ppermute | solution.py:10
  109.5 11.1 %collective-permute-start.10 = (bf16[128,2048]{1,0:T(8,128)(2,1)S(1)}, bf16[128,2048]{1,0:T(8,128)(2,1)S(1)}, u32[]{:S(2)}, u32[]{:S(2)}) collective-permute-start(bf16[128,2048]{1,0:T(8,128)(2,1)S(1)} %fusion.252), channel_id=1, source_target_pairs={{0,8},{1,9},{2,10},{3,11},{4,12},{5,13},{6,14},{7,15},{8,16},{9,17... | collective-permute-start | bytes 1572872 | tf_op jit(solution)/shard_map/ppermute | solution.py:10
  121.5 22.6 %collective-permute-start.11 = (bf16[128,2048]{1,0:T(8,128)(2,1)S(1)}, bf16[128,2048]{1,0:T(8,128)(2,1)S(1)}, u32[]{:S(2)}, u32[]{:S(2)}) collective-permute-start(bf16[128,2048]{1,0:T(8,128)(2,1)S(1)} %fusion.254), channel_id=1, source_target_pairs={{0,16},{1,17},{2,18},{3,19},{4,20},{5,21},{6,22},{7,23},{8,24},{9,... | collective-permute-start | bytes 1572872 | tf_op jit(solution)/shard_map/ppermute | solution.py:10
  145.0 42.4 %collective-permute-start.12 = (bf16[128,2048]{1,0:T(8,128)(2,1)S(1)}, bf16[128,2048]{1,0:T(8,128)(2,1)S(1)}, u32[]{:S(2)}, u32[]{:S(2)}) collective-permute-start(bf16[128,2048]{1,0:T(8,128)(2,1)S(1)} %fusion.256), channel_id=1, source_target_pairs={{0,32},{1,33},{2,34},{3,35},{4,36},{5,37},{6,38},{7,39},{8,40},{9,... | collective-permute-start | bytes 1572872 | tf_op jit(solution)/shard_map/ppermute | solution.py:10
  205.2 478.1 %all-reduce.2.cloned.1.call-start = ((), (), s32[]{:S(2)}) async-start(), calls=%async_computation.2 | async-start | bytes 262144 | tf_op jit(solution)/shard_map/psum | solution.py:106
  206.5 20.8 %collective-permute-start.13 = (bf16[128,2048]{1,0:T(8,128)(2,1)S(1)}, bf16[128,2048]{1,0:T(8,128)(2,1)S(1)}, u32[]{:S(2)}, u32[]{:S(2)}) collective-permute-start(bf16[128,2048]{1,0:T(8,128)(2,1)S(1)} %fusion.189), channel_id=1, source_target_pairs={{32,0},{33,1},{34,2},{35,3},{36,4},{37,5},{38,6},{39,7},{40,8},{41... | collective-permute-start | bytes 1572872 | tf_op jit(solution)/shard_map/ppermute | solution.py:10
  229.3 27.5 %collective-permute-start.14 = (bf16[128,2048]{1,0:T(8,128)(2,1)S(1)}, bf16[128,2048]{1,0:T(8,128)(2,1)S(1)}, u32[]{:S(2)}, u32[]{:S(2)}) collective-permute-start(bf16[128,2048]{1,0:T(8,128)(2,1)S(1)} %fusion.182), channel_id=1, source_target_pairs={{16,0},{17,1},{18,2},{19,3},{20,4},{21,5},{22,6},{23,7},{24,8},{25... | collective-permute-start | bytes 1572872 | tf_op jit(solution)/shard_map/ppermute | solution.py:10
  259.0 15.1 %collective-permute-start.15 = (bf16[128,2048]{1,0:T(8,128)(2,1)S(1)}, bf16[128,2048]{1,0:T(8,128)(2,1)S(1)}, u32[]{:S(2)}, u32[]{:S(2)}) collective-permute-start(bf16[128,2048]{1,0:T(8,128)(2,1)S(1)} %fusion.175), channel_id=1, source_target_pairs={{8,0},{9,1},{10,2},{11,3},{12,4},{13,5},{14,6},{15,7},{16,8},{17,9... | collective-permute-start | bytes 1572872 | tf_op jit(solution)/shard_map/ppermute | solution.py:10
  278.5 21.1 %collective-permute-start.16 = (bf16[128,2048]{1,0:T(8,128)(2,1)S(1)}, bf16[128,2048]{1,0:T(8,128)(2,1)S(1)}, u32[]{:S(2)}, u32[]{:S(2)}) collective-permute-start(bf16[128,2048]{1,0:T(8,128)(2,1)S(1)} %get-tuple-element.56), channel_id=1, source_target_pairs={{4,0},{5,1},{6,2},{7,3},{8,4},{9,5},{10,6},{11,7},{12,8},{13,9},{1... | collective-permute-start | bytes 1572872 | tf_op jit(solution)/shard_map/ppermute | solution.py:10
  303.0 33.5 %collective-permute-start.17 = (bf16[128,2048]{1,0:T(8,128)(2,1)S(1)}, bf16[128,2048]{1,0:T(8,128)(2,1)S(1)}, u32[]{:S(2)}, u32[]{:S(2)}) collective-permute-start(bf16[128,2048]{1,0:T(8,128)(2,1)S(1)} %get-tuple-element.57), channel_id=1, source_target_pairs={{2,0},{3,1},{4,2},{5,3},{6,4},{7,5},{8,6},{9,7},{10,8},{11,9},{12,... | collective-permute-start | bytes 1572872 | tf_op jit(solution)/shard_map/ppermute | solution.py:10
  339.9 8.6 %collective-permute-start.18 = (bf16[128,2048]{1,0:T(8,128)(2,1)S(1)}, bf16[128,2048]{1,0:T(8,128)(2,1)S(1)}, u32[]{:S(2)}, u32[]{:S(2)}) collective-permute-start(bf16[128,2048]{1,0:T(8,128)(2,1)S(1)} %get-tuple-element.58), channel_id=1, source_target_pairs={{1,0},{2,1},{3,2},{4,3},{5,4},{6,5},{7,6},{8,7},{9,8},{10,9},{11,1... | collective-permute-start | bytes 1572872 | tf_op jit(solution)/shard_map/ppermute | solution.py:10
  351.2 8.1 %collective-permute-start.19 = (bf16[64,2048]{1,0:T(8,128)(2,1)S(1)}, bf16[64,2048]{1,0:T(8,128)(2,1)S(1)}, u32[]{:S(2)}, u32[]{:S(2)}) collective-permute-start(bf16[64,2048]{1,0:T(8,128)(2,1)S(1)} %get-tuple-element.67), channel_id=1, source_target_pairs={{1,0},{2,1},{3,2},{4,3},{5,4},{6,5},{7,6},{8,7},{9,8},{10,9},{11,1... | collective-permute-start | bytes 786440 | tf_op jit(solution)/shard_map/ppermute | solution.py:10
  361.8 9.0 %collective-permute-start.20 = (bf16[32,2048]{1,0:T(8,128)(2,1)S(1)}, bf16[32,2048]{1,0:T(8,128)(2,1)S(1)}, u32[]{:S(2)}, u32[]{:S(2)}) collective-permute-start(bf16[32,2048]{1,0:T(8,128)(2,1)S(1)} %slice.215), channel_id=1, source_target_pairs={{1,0},{2,1},{3,2},{4,3},{5,4},{6,5},{7,6},{8,7},{9,8},{10,9},{11,1... | collective-permute-start | bytes 393224 | tf_op jit(solution)/shard_map/ppermute | solution.py:10
  372.8 8.2 %collective-permute-start.21 = (bf16[16,2048]{1,0:T(8,128)(2,1)S(1)}, bf16[16,2048]{1,0:T(8,128)(2,1)S(1)}, u32[]{:S(2)}, u32[]{:S(2)}) collective-permute-start(bf16[16,2048]{1,0:T(8,128)(2,1)S(1)} %slice.217), channel_id=1, source_target_pairs={{1,0},{2,1},{3,2},{4,3},{5,4},{6,5},{7,6},{8,7},{9,8},{10,9},{11,1... | collective-permute-start | bytes 196616 | tf_op jit(solution)/shard_map/ppermute | solution.py:10
  383.0 5.5 collective-permute-start.22
  390.6 5.2 collective-permute-start.23
  398.2 5.9 collective-permute-start.24
  402.6 111.1 %copy-start.28 = (f32[1,2048]{1,0:T(1,128)S(1)}, f32[1,2048]{1,0:T(1,128)}, u32[]{:S(2)}) copy-start(f32[1,2048]{1,0:T(1,128)} %get-tuple-element.84) | copy-start | bytes 24580
  406.3 107.4 %collective-permute-start.25 = (bf16[1,2048]{1,0:T(2,128)(2,1)S(1)}, bf16[1,2048]{1,0:T(2,128)(2,1)S(1)}, u32[]{:S(2)}, u32[]{:S(2)}) collective-permute-start(bf16[1,2048]{1,0:T(2,128)(2,1)S(1)} %slice.225), channel_id=1, source_target_pairs={{1,0},{2,1},{3,2},{4,3},{5,4},{6,5},{7,6},{8,7},{9,8},{10,9},{11,1... | collective-permute-start | bytes 12296 | tf_op jit(solution)/shard_map/ppermute | solution.py:10
  409.8 275.1 %all-gather.3.cloned.1.call-start = ((), (), s32[]{:S(2)}) async-start(), calls=%async_computation.3 | async-start | bytes 1310720 | tf_op jit(solution)/shard_map/all_gather | solution.py:115
  (100 other events, 4152.5 us)
Sparse Core Ops, SparseCore 0:
  205.3 223.5 reduce-scatter.1
  430.8 36.2 all-gather.2
Sparse Core Ops, SparseCore 1:
  409.9 273.3 all-reduce.1
